TPU v7x, 32 devices: a whole 2x2x4 slice. The times are simulated.
32 devices in a mesh: expert: 8 (over y, x, core), dp: 4 (over z).
Axes of the slice: x: 2, y: 2, z: 4, core: 2. Of those that a mesh axis runs over, the one named last changes fastest.
Arguments:
- tokens: bfloat16 [512, 2048], P(('expert', 'dp')), may hold values from -6 to 6
- out_grad: bfloat16 [512, 2048], P(('expert', 'dp')), may hold values from -6 to 6
- routes: int32 [512, 8], P(('expert', 'dp')), may hold values from 0 to 15, all different within a row; in each aligned block of 16 rows (0 to 15, 16 to 31, ...) at most 16 rows name the same one
- route_gates: float32 [512, 8], P(('expert', 'dp')), may hold values from 0.05 to 0.5
- w_gate: bfloat16 [16, 2048, 384], P('expert'), may hold values from -0.125 to 0.125
- w_up: bfloat16 [16, 2048, 384], P('expert'), may hold values from -0.125 to 0.125
- w_down: bfloat16 [16, 384, 2048], P('expert'), may hold values from -0.3125 to 0.3125
Outputs:
- token_grad: bfloat16 [512, 2048], P(('expert', 'dp'))
- down_grad: float32 [384, 16, 2048], P('dp', 'expert')
Inputs may be any that keep to these rules, and one draw needn't show every extreme that they name: `routes`: each row names 8 different experts. Among the 16 tokens of one device no expert is named more than 16 times, a bound that some block reaches.
All inputs are finite; a program needn't handle non-finite values.
Results may differ from a plain program's by a relative error of at most 0.014.
Values may be sent and summed in bfloat16 or wider, within the bound.
A program may use at most 64 MiB of HBM per device.

v0:
```python
import jax
import jax.numpy as jnp
from jax import lax
from jax.sharding import PartitionSpec as P


def gate_up(arrived, w_gate, w_up):
    gate_pre = jnp.einsum("erd,edf->erf", arrived, w_gate, preferred_element_type=jnp.float32)
    up_pre = jnp.einsum("erd,edf->erf", arrived, w_up, preferred_element_type=jnp.float32)
    return (gate_pre, up_pre)


def shards(tokens, out_grad, routes, route_gates, w_gate, w_up, w_down):
    tok_count, model_width = tokens.shape
    top_count = routes.shape[1]
    local_experts = w_gate.shape[0]
    groups = lax.axis_size("expert")
    experts = local_experts * groups
    slot_count = 2 * tok_count * top_count // experts
    flat_routes = routes.reshape(-1)
    onehot = (flat_routes[:, None] == jnp.arange(experts, dtype=jnp.int32)[None, :]).astype(
        jnp.int32
    )
    slot_rank = jnp.sum(onehot * (jnp.cumsum(onehot, axis=0) - onehot), axis=1)
    slot_index = flat_routes * slot_count + slot_rank
    placement = slot_index[None, :] == jnp.arange(experts * slot_count, dtype=jnp.int32)[:, None]
    route_place = placement.astype(jnp.bfloat16)
    token_place = jnp.sum(
        placement.reshape(experts * slot_count, tok_count, top_count).astype(jnp.float32), axis=2
    ).astype(jnp.bfloat16)
    send_inputs = (
        jnp.dot(token_place, tokens, preferred_element_type=jnp.float32)
        .astype(jnp.bfloat16)
        .reshape(experts, slot_count, model_width)
    )
    scaled = (
        (route_gates[:, :, None] * out_grad[:, None, :].astype(jnp.float32))
        .astype(jnp.bfloat16)
        .reshape(tok_count * top_count, model_width)
    )
    send_grads = (
        jnp.dot(route_place, scaled, preferred_element_type=jnp.float32)
        .astype(jnp.bfloat16)
        .reshape(experts, slot_count, model_width)
    )
    arrived, arrived_grad = (
        lax.all_to_all(send_inputs, "expert", split_axis=0, concat_axis=1, tiled=True),
        lax.all_to_all(send_grads, "expert", split_axis=0, concat_axis=1, tiled=True),
    )
    gate_pre, up_pre = gate_up(arrived, w_gate, w_up)
    sigmoid_gate = jax.nn.sigmoid(gate_pre)
    silu_gate = gate_pre * sigmoid_gate
    hidden = (silu_gate * up_pre).astype(jnp.bfloat16)
    hidden_grad = jnp.einsum(
        "erd,efd->erf", arrived_grad, w_down, preferred_element_type=jnp.float32
    )
    gate_grad = (
        hidden_grad * up_pre * (sigmoid_gate + gate_pre * sigmoid_gate * (1.0 - sigmoid_gate))
    ).astype(jnp.bfloat16)
    up_grad = (hidden_grad * silu_gate).astype(jnp.bfloat16)
    row_grads = (
        jnp.einsum("erf,edf->erd", gate_grad, w_gate, preferred_element_type=jnp.float32)
        + jnp.einsum("erf,edf->erd", up_grad, w_up, preferred_element_type=jnp.float32)
    ).astype(jnp.bfloat16)
    returned = lax.all_to_all(row_grads, "expert", split_axis=1, concat_axis=0, tiled=True)
    token_grad = lax.dot_general(
        token_place,
        returned.reshape(experts * slot_count, model_width),
        (((0,), (0,)), ((), ())),
        preferred_element_type=jnp.float32,
    ).astype(jnp.bfloat16)
    hidden_units = hidden.shape[2]
    share_rows = hidden_units // lax.axis_size("dp")
    partial_grad = jnp.einsum(
        "erf,erd->fed", hidden, arrived_grad, preferred_element_type=jnp.float32
    ).astype(jnp.bfloat16)
    total_grad = lax.psum(partial_grad, "dp").astype(jnp.float32)
    first_row = lax.axis_index("dp") * share_rows
    down_grad = lax.dynamic_slice_in_dim(total_grad, first_row, share_rows, 0)
    return (token_grad, down_grad)


def solution(mesh):
    placed = (
        P(("expert", "dp"), None),
        P(("expert", "dp"), None),
        P(("expert", "dp"), None),
        P(("expert", "dp"), None),
        P("expert", None, None),
        P("expert", None, None),
        P("expert", None, None),
    )
    return jax.shard_map(
        shards,
        mesh=mesh,
        in_specs=placed,
        out_specs=(P(("expert", "dp"), None), P("dp", "expert", None)),
        check_vma=False,
    )
```

profile of v0, /device:TPU:0, one launch (start us, length us, event | category | flops | bytes accessed | tf_op | source)
XLA Modules:
  0.0 193.7 jit_solution(11863418635343941623)
XLA Ops:
  7.2 0.0 copy-start
  7.2 0.0 copy-start.6
  7.2 0.9 copy.42
  8.1 0.1 eq.35
  8.2 0.1 fusion.10
  8.3 0.2 reduce_window_sum.11
  8.5 0.2 select_reduce_fusion
  8.7 0.9 convert_element_type.51
  9.5 0.8 copy.44
  10.3 0.1 mul.63
  10.4 1.5 convolution_convert_fusion.1
  11.8 5.2 %all-to-all-start = ((bf16[16,16,2048]{2,1,0:T(8,128)(2,1)}), bf16[16,16,2048]{2,1,0:T(8,128)(2,1)}, u32[]{:S(2)}, u32[]{:S(2)}) async-start(bf16[16,16,2048]{2,1,0:T(8,128)(2,1)} %bitcast.38), calls=%async_computation | async-start | bytes 2097152 | tf_op jit(solution)/shard_map/all_to_all | solution.py:48
  17.0 0.1 reduce_sum.21
  17.1 0.1 convert_reduce_fusion
  17.3 0.0 copy-done.6
  17.3 1.5 convolution_convert_fusion.2
  18.7 13.8 %all-to-all-done = bf16[16,16,2048]{2,1,0:T(8,128)(2,1)} async-done(((bf16[16,16,2048]{2,1,0:T(8,128)(2,1)}), bf16[16,16,2048]{2,1,0:T(8,128)(2,1)}, u32[]{:S(2)}, u32[]{:S(2)}) %all-to-all-start) | async-done | bytes 1048608 | tf_op jit(solution)/shard_map/all_to_all | solution.py:48
  32.5 4.2 %all-to-all-start.1 = ((bf16[16,16,2048]{2,1,0:T(8,128)(2,1)}), bf16[16,16,2048]{2,1,0:T(8,128)(2,1)}, u32[]{:S(2)}, u32[]{:S(2)}) async-start(bf16[16,16,2048]{2,1,0:T(8,128)(2,1)} %bitcast.39), calls=%async_computation.1 | async-start | bytes 2097152 | tf_op jit(solution)/shard_map/all_to_all | solution.py:47
  36.8 0.0 all-reduce.2.cloned.1.call-start
  36.8 2.3 %copy.45 = bf16[8,2,16,2048]{3,2,0,1:T(8,128)(2,1)} copy(bf16[8,2,16,2048]{3,2,1,0:T(8,128)(2,1)} %bitcast.2) | data formatting | bytes 2097152 | tf_op jit(solution)/shard_map/all_to_all | solution.py:48
  39.1 13.0 %all-to-all-done.1 = bf16[16,16,2048]{2,1,0:T(8,128)(2,1)} async-done(((bf16[16,16,2048]{2,1,0:T(8,128)(2,1)}), bf16[16,16,2048]{2,1,0:T(8,128)(2,1)}, u32[]{:S(2)}, u32[]{:S(2)}) %all-to-all-start.1) | async-done | bytes 1048608 | tf_op jit(solution)/shard_map/all_to_all | solution.py:47
  52.2 0.0 copy-start.1
  52.2 1.5 copy.46
  53.6 0.0 copy-done
  53.7 0.8 fusion.19
  54.4 0.0 copy-done.1
  54.4 0.0 copy-start.3
  54.4 0.7 fusion.18
  55.1 0.0 copy-start.4
  55.2 0.8 copy-done.4
  55.9 0.0 copy-done.3
  55.9 2.7 %fusion = bf16[384,2,2048]{0,2,1:T(8,128)(2,1)} fusion(bf16[2,128,2048]{2,1,0:T(8,128)(2,1)S(1)} %bitcast.35, f32[2,128,384]{2,1,0:T(8,128)S(1)} %fusion.18, f32[2,128,384]{2,1,0:T(8,128)S(1)} %fusion.19), kind=kOutput, calls=%fused_computation.1 | convolution fusion | flops 404815872 | bytes 4980736 | tf_op jit(solution)/shard_map/erf,erd->fed/dot_general | solution.py:74
  58.6 0.0 all-reduce.2.cloned.1.call-update
  58.6 0.0 copy-start.5
  58.7 3.3 %fusion.17 = f32[2,128,384]{2,1,0:T(8,128)S(1)} fusion(bf16[2,128,2048]{2,1,0:T(8,128)(2,1)} %bitcast.34, bf16[2,384,2048]{2,1,0:T(8,128)(2,1)} %param.13), kind=kOutput, calls=%fused_computation.31 | convolution fusion | flops 402653184 | bytes 4587520 | tf_op jit(solution)/shard_map/erd,efd->erf/dot_general | solution.py:54
  62.0 0.0 copy-done.5
  62.0 0.0 copy-start.2
  62.0 1.1 fusion.7
  63.1 0.8 copy-done.2
  63.9 1.1 fusion.1
  65.0 2.0 %copy.47 = bf16[2,128,2048]{2,0,1:T(2,128)(2,1)} copy(bf16[2,128,2048]{2,1,0:T(8,128)(2,1)S(1)} %fusion.1) | data formatting | bytes 2097152 | tf_op jit(solution)/shard_map/convert_element_type | solution.py:64
  67.1 4.2 %all-to-all-start.2 = ((bf16[2,128,2048]{2,0,1:T(2,128)(2,1)}), bf16[2,128,2048]{2,0,1:T(2,128)(2,1)}, u32[]{:S(2)}, u32[]{:S(2)}) async-start(bf16[2,128,2048]{2,0,1:T(2,128)(2,1)} %copy.47), calls=%async_computation.2 | async-start | bytes 2097152 | tf_op jit(solution)/shard_map/all_to_all | solution.py:65
  71.3 15.4 %all-to-all-done.2 = bf16[2,128,2048]{2,0,1:T(2,128)(2,1)} async-done(((bf16[2,128,2048]{2,0,1:T(2,128)(2,1)}), bf16[2,128,2048]{2,0,1:T(2,128)(2,1)}, u32[]{:S(2)}, u32[]{:S(2)}) %all-to-all-start.2) | async-done | bytes 1048608 | tf_op jit(solution)/shard_map/all_to_all | solution.py:65
  86.7 1.6 copy.48
  88.3 0.1 copy.49
  88.4 0.9 convolution_convert_fusion.3
  89.3 90.4 %all-reduce.2.cloned.1.call-done = bf16[384,2,2048]{0,2,1:T(8,128)(2,1)} async-done(((bf16[384,2,2048]{0,2,1:T(8,128)(2,1)}), bf16[384,2,2048]{0,2,1:T(8,128)(2,1)}) %all-reduce.2.cloned.1.call-update) | async-done | bytes 3145744 | tf_op jit(solution)/shard_map/psum | solution.py:77
  179.7 3.3 %dynamic-slice_convert_fusion = f32[96,2,2048]{0,2,1:T(8,128)} fusion(bf16[384,2,2048]{0,2,1:T(8,128)(2,1)} %all-reduce.2.cloned.1.call-done, s32[]{:T(128)S(6)} %select_n.3), kind=kLoop, calls=%fused_computation.7 | loop fusion | flops 393216 | bytes 2359300 | tf_op jit(solution)/shard_map/convert_element_type | solution.py:77
  183.0 3.9 %copy.51 = f32[96,2,2048]{2,1,0:T(2,128)} copy(f32[96,2,2048]{0,2,1:T(8,128)} %dynamic-slice_convert_fusion) | data formatting | bytes 3145728
  (2 shorter events, 0.0 us)
Async XLA Ops:
  7.2 46.5 %copy-start = (bf16[2,2048,384]{2,1,0:T(8,128)(2,1)S(1)}, bf16[2,2048,384]{2,1,0:T(8,128)(2,1)}, u32[]{:S(2)}) copy-start(bf16[2,2048,384]{2,1,0:T(8,128)(2,1)} %param.11) | copy-start | bytes 9437188
  7.2 10.1 %copy-start.6 = (bf16[16,2048]{1,0:T(8,128)(2,1)S(1)}, bf16[16,2048]{1,0:T(8,128)(2,1)}, u32[]{:S(2)}) copy-start(bf16[16,2048]{1,0:T(8,128)(2,1)} %param.7) | copy-start | bytes 196612
  11.8 20.7 %all-to-all-start = ((bf16[16,16,2048]{2,1,0:T(8,128)(2,1)}), bf16[16,16,2048]{2,1,0:T(8,128)(2,1)}, u32[]{:S(2)}, u32[]{:S(2)}) async-start(bf16[16,16,2048]{2,1,0:T(8,128)(2,1)} %bitcast.38), calls=%async_computation | async-start | bytes 2097152 | tf_op jit(solution)/shard_map/all_to_all | solution.py:48
  32.5 19.6 %all-to-all-start.1 = ((bf16[16,16,2048]{2,1,0:T(8,128)(2,1)}), bf16[16,16,2048]{2,1,0:T(8,128)(2,1)}, u32[]{:S(2)}, u32[]{:S(2)}) async-start(bf16[16,16,2048]{2,1,0:T(8,128)(2,1)} %bitcast.39), calls=%async_computation.1 | async-start | bytes 2097152 | tf_op jit(solution)/shard_map/all_to_all | solution.py:47
  36.8 142.9 %all-reduce.2.cloned.1.call-start = ((), (), s32[]{:S(2)}) async-start(), calls=%async_computation.3 | async-start | bytes 6291456 | tf_op jit(solution)/shard_map/psum | solution.py:77
  52.2 2.3 %copy-start.1 = (bf16[2,2048,384]{2,1,0:T(8,128)(2,1)S(1)}, bf16[2,2048,384]{2,1,0:T(8,128)(2,1)}, u32[]{:S(2)}) copy-start(bf16[2,2048,384]{2,1,0:T(8,128)(2,1)} %param.12) | copy-start | bytes 9437188
  54.4 1.5 copy-start.3
  55.1 0.8 copy-start.4
  58.6 3.3 %copy-start.5 = (f32[2,128,384]{2,1,0:T(8,128)S(1)}, f32[2,128,384]{2,1,0:T(8,128)}, u32[]{:S(2)}) copy-start(f32[2,128,384]{2,1,0:T(8,128)} %copy-done.4) | copy-start | bytes 1179652
  62.0 1.9 copy-start.2
  67.1 19.6 %all-to-all-start.2 = ((bf16[2,128,2048]{2,0,1:T(2,128)(2,1)}), bf16[2,128,2048]{2,0,1:T(2,128)(2,1)}, u32[]{:S(2)}, u32[]{:S(2)}) async-start(bf16[2,128,2048]{2,0,1:T(2,128)(2,1)} %copy.47), calls=%async_computation.2 | async-start | bytes 2097152 | tf_op jit(solution)/shard_map/all_to_all | solution.py:65
Sparse Core Ops, SparseCore 0:
  58.8 120.8 all-reduce.1
where the time goes:
time: 194 us
  waiting for transfers between devices  133 us (69%)
  local copies, waits for them, and re-layouts  14.9 us (8%)
  between operations  14.2 us (7%)
  starting transfers between devices  13.7 us (7%)
  matrix products  13.5 us (7%)
  other arithmetic  4.72 us (2%)
    psum x1, waiting for transfers between devices, shards(): total_grad = lax.psum(partial_grad, 'dp').astype(jnp.float32)  90.4 us
    all_to_all x1, waiting for transfers between devices, shards(): lax.all_to_all(row_grads, 'expert', split_axis=1, concat_axis=0, tiled=True)  15.4 us
    all_to_all x1, waiting for transfers between devices, shards(): lax.all_to_all(send_grads, 'expert', split_axis=0, concat_axis=1, tiled=T...  13.8 us
    all_to_all x1, waiting for transfers between devices, shards(): lax.all_to_all(send_inputs, 'expert', split_axis=0, concat_axis=1, tiled=...  13 us
    unnamed x17, local copies, waits for them, and re-layouts  7.11 us
    all_to_all x1, starting transfers between devices, shards(): lax.all_to_all(send_grads, 'expert', split_axis=0, concat_axis=1, tiled=T...  5.2 us
    all_to_all x1, starting transfers between devices, shards(): lax.all_to_all(row_grads, 'expert', split_axis=1, concat_axis=0, tiled=True)  4.25 us
    all_to_all x1, starting transfers between devices, shards(): lax.all_to_all(send_inputs, 'expert', split_axis=0, concat_axis=1, tiled=...  4.24 us
  transfers between devices with their start and end apart: 4, of which 4 were waited for; matrix products, arithmetic and copies ran while one was open for 7% of the time, Pallas kernels for 0%

commit v1 on v0

--- a/solution.py
+++ b/solution.py
@@ -2,6 +2,13 @@
 import jax.numpy as jnp
 from jax import lax
 from jax.sharding import PartitionSpec as P
+
+
+def stacked_exchange(value, name, split, join):
+    size = lax.axis_size(name)
+    parts = jnp.stack(jnp.split(value, size, axis=split), axis=0)
+    parts = lax.all_to_all(parts, name, split_axis=0, concat_axis=0)
+    return jnp.concatenate(parts, axis=join)
 
 
 def gate_up(arrived, w_gate, w_up):
@@ -45,7 +52,7 @@
     )
     arrived, arrived_grad = (
         lax.all_to_all(send_inputs, "expert", split_axis=0, concat_axis=1, tiled=True),
-        lax.all_to_all(send_grads, "expert", split_axis=0, concat_axis=1, tiled=True),
+        stacked_exchange(send_grads, "expert", 0, 1),
     )
     gate_pre, up_pre = gate_up(arrived, w_gate, w_up)
     sigmoid_gate = jax.nn.sigmoid(gate_pre)

time: 194 us -> 200 us (1.031)
  local copies, waits for them, and re-layouts: 14.9 us -> 19.8 us
    unnamed x17 -> x22, local copies, waits for them, and re-layouts: 7.11 us -> 11.4 us
    all_to_all x1 -> x0, local copies, waits for them, and re-layouts: 2.3 us -> none  [shards(): lax.all_to_all(send_grads, 'expert', split_axis=0, concat_axis=1, tiled=T...]
    reshape x0 -> x1, local copies, waits for them, and re-layouts: none -> 2.3 us  [stacked_exchange(): return jnp.concatenate(parts, axis=join)]
where the time goes in v1:
time: 200 us
  waiting for transfers between devices  133 us (66%)
  local copies, waits for them, and re-layouts  19.8 us (10%)
  matrix products  14.5 us (7%)
  between operations  14.2 us (7%)
  starting transfers between devices  13.7 us (7%)
  other arithmetic  4.87 us (2%)
    psum x1, waiting for transfers between devices, shards(): total_grad = lax.psum(partial_grad, 'dp').astype(jnp.float32)  90.4 us
    all_to_all x1, waiting for transfers between devices, shards(): lax.all_to_all(row_grads, 'expert', split_axis=1, concat_axis=0, tiled=True)  15.4 us
    all_to_all x1, waiting for transfers between devices, stacked_exchange(): parts = lax.all_to_all(parts, name, split_axis=0, concat_axis=0)  13.8 us
    all_to_all x1, waiting for transfers between devices, shards(): lax.all_to_all(send_inputs, 'expert', split_axis=0, concat_axis=1, tiled=...  13 us
    unnamed x22, local copies, waits for them, and re-layouts  11.4 us
    all_to_all x1, starting transfers between devices, stacked_exchange(): parts = lax.all_to_all(parts, name, split_axis=0, concat_axis=0)  5.2 us
    all_to_all x1, starting transfers between devices, shards(): lax.all_to_all(row_grads, 'expert', split_axis=1, concat_axis=0, tiled=True)  4.25 us
    all_to_all x1, starting transfers between devices, shards(): lax.all_to_all(send_inputs, 'expert', split_axis=0, concat_axis=1, tiled=...  4.24 us
  transfers between devices with their start and end apart: 4, of which 4 were waited for; matrix products, arithmetic and copies ran while one was open for 7% of the time, Pallas kernels for 0%

profile of v1, /device:TPU:0, one launch (start us, length us, event | category | flops | bytes accessed | tf_op | source)
XLA Modules:
  0.0 199.7 jit_solution(2761367464395718994)
XLA Ops:
  7.2 0.0 copy-start
  7.2 1.0 convert_element_type.51
  8.2 0.8 copy.44
  8.9 0.1 mul.63
  9.0 0.8 copy.42
  9.8 0.1 eq.35
  9.9 0.1 fusion.10
  10.0 0.2 reduce_window_sum.11
  10.2 0.2 select_reduce_fusion
  10.3 0.5 convolution_convert_fusion.1
  10.8 0.0 copy-start.5
  10.9 0.1 fusion.17
  10.9 0.7 constant_dynamic-update-slice_fusion.7
  11.6 0.7 constant_dynamic-update-slice_fusion.6
  12.3 0.7 constant_dynamic-update-slice_fusion.5
  12.9 0.7 constant_dynamic-update-slice_fusion.4
  13.6 0.7 constant_dynamic-update-slice_fusion.3
  14.3 0.7 constant_dynamic-update-slice_fusion.2
  14.9 0.7 constant_dynamic-update-slice_fusion.1
  15.6 0.7 constant_dynamic-update-slice_fusion
  16.2 5.2 %all-to-all-start = ((bf16[8,2,16,2048]{3,2,1,0:T(8,128)(2,1)}), bf16[8,2,16,2048]{3,2,1,0:T(8,128)(2,1)}, u32[]{:S(2)}, u32[]{:S(2)}) async-start(bf16[8,2,16,2048]{3,2,1,0:T(8,128)(2,1)} %constant_dynamic-update-slice_fusion), calls=%async_computation | async-start | bytes 2097152 | tf_op jit(solution)/shard_map/all_to_all | solution.py:10
  21.4 0.1 reduce_sum.21
  21.5 0.1 convert_reduce_fusion
  21.7 0.0 copy-done.5
  21.7 1.5 convolution_convert_fusion.2
  23.1 13.8 %all-to-all-done = bf16[8,2,16,2048]{3,2,1,0:T(8,128)(2,1)} async-done(((bf16[8,2,16,2048]{3,2,1,0:T(8,128)(2,1)}), bf16[8,2,16,2048]{3,2,1,0:T(8,128)(2,1)}, u32[]{:S(2)}, u32[]{:S(2)}) %all-to-all-start) | async-done | bytes 1048608 | tf_op jit(solution)/shard_map/all_to_all | solution.py:10
  36.9 4.2 %all-to-all-start.1 = ((bf16[16,16,2048]{2,1,0:T(8,128)(2,1)}), bf16[16,16,2048]{2,1,0:T(8,128)(2,1)}, u32[]{:S(2)}, u32[]{:S(2)}) async-start(bf16[16,16,2048]{2,1,0:T(8,128)(2,1)} %bitcast.43), calls=%async_computation.1 | async-start | bytes 2097152 | tf_op jit(solution)/shard_map/all_to_all | solution.py:54
  41.2 0.0 all-reduce.2.cloned.1.call-start
  41.2 2.3 %copy.45 = bf16[2,8,16,2048]{3,2,1,0:T(8,128)(2,1)} copy(bf16[2,8,16,2048]{3,2,0,1:T(8,128)(2,1)} %bitcast.9) | data formatting | bytes 2097152 | tf_op jit(solution)/shard_map/reshape | solution.py:11
  43.5 13.0 %all-to-all-done.1 = bf16[16,16,2048]{2,1,0:T(8,128)(2,1)} async-done(((bf16[16,16,2048]{2,1,0:T(8,128)(2,1)}), bf16[16,16,2048]{2,1,0:T(8,128)(2,1)}, u32[]{:S(2)}, u32[]{:S(2)}) %all-to-all-start.1) | async-done | bytes 1048608 | tf_op jit(solution)/shard_map/all_to_all | solution.py:54
  56.6 1.3 copy.46
  57.9 2.7 %fusion.19 = f32[2,128,384]{2,1,0:T(8,128)S(1)} fusion(bf16[2,128,2048]{2,1,0:T(8,128)(2,1)S(1)} %bitcast.41, bf16[2,2048,384]{2,1,0:T(8,128)(2,1)} %param.12), kind=kOutput, calls=%fused_computation.41 | convolution fusion | flops 402653184 | bytes 4587520 | tf_op jit(solution)/shard_map/erd,edf->erf/dot_general | solution.py:16
  60.6 0.0 copy-done
  60.6 0.0 copy-start.3
  60.6 0.0 copy-start.2
  60.6 0.8 fusion.20
  61.3 0.0 copy-done.3
  61.4 0.6 copy-done.2
  61.9 2.7 %fusion = bf16[384,2,2048]{0,2,1:T(8,128)(2,1)} fusion(bf16[2,128,2048]{2,1,0:T(8,128)(2,1)S(1)} %bitcast.40, f32[2,128,384]{2,1,0:T(8,128)S(1)} %fusion.19, f32[2,128,384]{2,1,0:T(8,128)S(1)} %fusion.20), kind=kOutput, calls=%fused_computation.1 | convolution fusion | flops 404815872 | bytes 4980736 | tf_op jit(solution)/shard_map/erf,erd->fed/dot_general | solution.py:81
  64.7 0.0 all-reduce.2.cloned.1.call-update
  64.7 0.0 copy-start.4
  64.7 3.3 %fusion.18 = f32[2,128,384]{2,1,0:T(8,128)S(1)} fusion(bf16[2,128,2048]{2,1,0:T(8,128)(2,1)} %bitcast.39, bf16[2,384,2048]{2,1,0:T(8,128)(2,1)} %param.13), kind=kOutput, calls=%fused_computation.40 | convolution fusion | flops 402653184 | bytes 4587520 | tf_op jit(solution)/shard_map/erd,efd->erf/dot_general | solution.py:61
  68.0 0.0 copy-done.4
  68.0 0.0 copy-start.1
  68.0 1.1 fusion.7
  69.2 0.8 copy-done.1
  69.9 1.1 fusion.1
  71.0 2.0 %copy.47 = bf16[2,128,2048]{2,0,1:T(2,128)(2,1)} copy(bf16[2,128,2048]{2,1,0:T(8,128)(2,1)S(1)} %fusion.1) | data formatting | bytes 2097152 | tf_op jit(solution)/shard_map/convert_element_type | solution.py:71
  73.1 4.2 %all-to-all-start.2 = ((bf16[2,128,2048]{2,0,1:T(2,128)(2,1)}), bf16[2,128,2048]{2,0,1:T(2,128)(2,1)}, u32[]{:S(2)}, u32[]{:S(2)}) async-start(bf16[2,128,2048]{2,0,1:T(2,128)(2,1)} %copy.47), calls=%async_computation.2 | async-start | bytes 2097152 | tf_op jit(solution)/shard_map/all_to_all | solution.py:72
  77.4 15.4 %all-to-all-done.2 = bf16[2,128,2048]{2,0,1:T(2,128)(2,1)} async-done(((bf16[2,128,2048]{2,0,1:T(2,128)(2,1)}), bf16[2,128,2048]{2,0,1:T(2,128)(2,1)}, u32[]{:S(2)}, u32[]{:S(2)}) %all-to-all-start.2) | async-done | bytes 1048608 | tf_op jit(solution)/shard_map/all_to_all | solution.py:72
  92.7 1.6 copy.48
  94.3 0.1 copy.49
  94.4 0.9 convolution_convert_fusion.3
  95.3 90.4 %all-reduce.2.cloned.1.call-done = bf16[384,2,2048]{0,2,1:T(8,128)(2,1)} async-done(((bf16[384,2,2048]{0,2,1:T(8,128)(2,1)}), bf16[384,2,2048]{0,2,1:T(8,128)(2,1)}) %all-reduce.2.cloned.1.call-update) | async-done | bytes 3145744 | tf_op jit(solution)/shard_map/psum | solution.py:84
  185.7 3.3 %dynamic-slice_convert_fusion = f32[96,2,2048]{0,2,1:T(8,128)} fusion(bf16[384,2,2048]{0,2,1:T(8,128)(2,1)} %all-reduce.2.cloned.1.call-done, s32[]{:T(128)S(6)} %select_n.3), kind=kLoop, calls=%fused_computation.7 | loop fusion | flops 393216 | bytes 2359300 | tf_op jit(solution)/shard_map/convert_element_type | solution.py:84
  189.0 3.9 %copy.51 = f32[96,2,2048]{2,1,0:T(2,128)} copy(f32[96,2,2048]{0,2,1:T(8,128)} %dynamic-slice_convert_fusion) | data formatting | bytes 3145728
  (2 shorter events, 0.0 us)
Async XLA Ops:
  7.2 53.4 %copy-start = (bf16[2,2048,384]{2,1,0:T(8,128)(2,1)S(1)}, bf16[2,2048,384]{2,1,0:T(8,128)(2,1)}, u32[]{:S(2)}) copy-start(bf16[2,2048,384]{2,1,0:T(8,128)(2,1)} %param.11) | copy-start | bytes 9437188
  10.8 10.8 %copy-start.5 = (bf16[16,2048]{1,0:T(8,128)(2,1)S(1)}, bf16[16,2048]{1,0:T(8,128)(2,1)}, u32[]{:S(2)}) copy-start(bf16[16,2048]{1,0:T(8,128)(2,1)} %param.7) | copy-start | bytes 196612
  16.2 20.7 %all-to-all-start = ((bf16[8,2,16,2048]{3,2,1,0:T(8,128)(2,1)}), bf16[8,2,16,2048]{3,2,1,0:T(8,128)(2,1)}, u32[]{:S(2)}, u32[]{:S(2)}) async-start(bf16[8,2,16,2048]{3,2,1,0:T(8,128)(2,1)} %constant_dynamic-update-slice_fusion), calls=%async_computation | async-start | bytes 2097152 | tf_op jit(solution)/shard_map/all_to_all | solution.py:10
  36.9 19.6 %all-to-all-start.1 = ((bf16[16,16,2048]{2,1,0:T(8,128)(2,1)}), bf16[16,16,2048]{2,1,0:T(8,128)(2,1)}, u32[]{:S(2)}, u32[]{:S(2)}) async-start(bf16[16,16,2048]{2,1,0:T(8,128)(2,1)} %bitcast.43), calls=%async_computation.1 | async-start | bytes 2097152 | tf_op jit(solution)/shard_map/all_to_all | solution.py:54
  41.2 144.5 %all-reduce.2.cloned.1.call-start = ((), (), s32[]{:S(2)}) async-start(), calls=%async_computation.3 | async-start | bytes 6291456 | tf_op jit(solution)/shard_map/psum | solution.py:84
  60.6 0.8 copy-start.3
  60.6 1.4 copy-start.2
  64.7 3.3 %copy-start.4 = (f32[2,128,384]{2,1,0:T(8,128)S(1)}, f32[2,128,384]{2,1,0:T(8,128)}, u32[]{:S(2)}) copy-start(f32[2,128,384]{2,1,0:T(8,128)} %copy-done.3) | copy-start | bytes 1179652
  68.0 1.9 copy-start.1
  73.1 19.6 %all-to-all-start.2 = ((bf16[2,128,2048]{2,0,1:T(2,128)(2,1)}), bf16[2,128,2048]{2,0,1:T(2,128)(2,1)}, u32[]{:S(2)}, u32[]{:S(2)}) async-start(bf16[2,128,2048]{2,0,1:T(2,128)(2,1)} %copy.47), calls=%async_computation.2 | async-start | bytes 2097152 | tf_op jit(solution)/shard_map/all_to_all | solution.py:72
Sparse Core Ops, SparseCore 0:
  64.8 120.8 all-reduce.1
